TPU v7x, 32 devices: a whole 2x2x4 slice. The times are simulated.
32 devices in a mesh: member: 8 (over z, core), basin: 4 (over y, x).
Axes of the slice: x: 2, y: 2, z: 4, core: 2. Of those that a mesh axis runs over, the one named last changes fastest.
Arguments:
- prior_params: float32 [256, 8, 512], P('member', None, 'basin'), may hold values from -3 to 3
- lateral_flow: float32 [256, 2, 65536], P('member', None, 'basin'), may hold values from 0.2 to 2
- inflow_start: float32 [65536], P('basin'), may hold values from 0.5 to 4
- outflow_start: float32 [65536], P('basin'), may hold values from 0.5 to 4
- reach_count: int32 [512], P('basin'), may hold values from 64 to 128
- downstream: int32 [512], P('basin'), may hold values from 0 to 63
- gauge_reach: int32 [2048], P('basin'), may hold values from 0 to 16383
- observed: float32 [2, 2048], P(None, 'basin'), may hold values from 0.5 to 4
- obs_var: float32 [2, 2048], P(None, 'basin'), may hold values from 0.02 to 0.5
- obs_noise: float32 [256, 2, 2048], P('member', None, 'basin'), may hold values from -4 to 4
Outputs:
- posterior: float32 [256, 8, 512], P('member', None, 'basin')
- predicted: float32 [256, 2, 2048], P('member', None, 'basin')
All inputs are finite; a program needn't handle non-finite values.
Results may differ from a plain program's by a relative error of at most 0.0003.
Values sent between devices are 32-bit elements; how exact they have to be, the bound alone decides.
A program may use at most 128 MiB of HBM per device.

v0:
```python
import math
import jax
import jax.numpy as jnp
from jax import lax
from jax.sharding import PartitionSpec as P

LANES = 128
BLK_LEV = 64
exact_mode = lax.Precision.HIGHEST


def shifted(block, axis, distance):
    devices = range(lax.axis_size(axis))
    route = [(i - distance, i) for i in devices if i - distance in devices]
    return lax.ppermute(block, axis, route)


def inverse_sinh(values):
    return jnp.log(values + jnp.sqrt(values * values + 1.0))


def route_coefficients(prior_params):
    storage = 0.02 + 0.1 * jax.nn.sigmoid(prior_params[:, 0, :])
    weighting = 0.2 * jax.nn.sigmoid(prior_params[:, 1, :])
    denominator = storage * (1.0 - weighting) + 0.5
    weight_now = (0.5 - storage * weighting) / denominator
    weight_back = (0.5 + storage * weighting) / denominator
    weight_carry = (storage * (1.0 - weighting) - 0.5) / denominator
    return (weight_now[:, :, None], weight_back[:, :, None], weight_carry[:, :, None])


def lateral_scaling(prior_params, lane_count):
    lane_pos = jnp.arange(lane_count, dtype=jnp.float32)
    orders = jnp.arange(6, dtype=jnp.float32)
    cosine_modes = jnp.cos(math.pi * orders[:, None] * (lane_pos[None, :] + 0.5) / lane_count)
    exponent = jnp.einsum(
        "mkb,kr->mbr", 0.2 * prior_params[:, 2:, :], cosine_modes, precision=exact_mode
    )
    return jnp.exp(exponent)


def solve_gram(gram_matrix, cross_matrix):
    factor = jnp.linalg.cholesky(gram_matrix)
    halfway = lax.linalg.triangular_solve(factor, cross_matrix, left_side=True, lower=True)
    return lax.linalg.triangular_solve(
        factor, halfway, left_side=True, lower=True, transpose_a=True
    )


def level_sweep(incoming, weights, lateral_now, live_mask, one_hot, prev_in, prev_out):
    weight_now, weight_back, weight_carry, scaling = weights
    level_blocks = one_hot[0].shape[0]
    upstream = incoming
    inflows = []
    outflows = []
    for level_idx in range(len(one_hot)):
        level_span = slice(level_idx * level_blocks, (level_idx + 1) * level_blocks)
        inflow = live_mask[level_span] * (
            lateral_now[:, level_span] * scaling[:, level_span] + upstream
        )
        outflow = (
            weight_now[:, level_span] * inflow
            + weight_back[:, level_span] * prev_in[:, level_span]
            + weight_carry[:, level_span] * prev_out[:, level_span]
        )
        upstream = jnp.einsum("nj,gjr->gnr", one_hot[level_idx], outflow, precision=exact_mode)
        inflows.append(inflow)
        outflows.append(outflow)
    return (jnp.concatenate(inflows, 1), jnp.concatenate(outflows, 1), upstream)


def route_hour(mover, groups, weights, lateral_now, live_mask, one_hot, prev_in, prev_out):
    members_dev, block_dev, lane_count = prev_in.shape
    level_blocks = one_hot[0].shape[0]
    group_size = members_dev // groups
    basins = lax.axis_size("basin")
    basin_idx = lax.axis_index("basin")

    def advance(step_idx, state_tuple):
        incoming, inflow_all, outflow_all = state_tuple
        group_idx = step_idx - basin_idx
        active = (group_idx >= 0) & (group_idx < groups)
        first_row = jnp.clip(group_idx, 0, groups - 1) * group_size

        def compute(operands):
            arriving, inflow_keep, outflow_keep = operands

            def take_group(values):
                return lax.dynamic_slice_in_dim(values, first_row, group_size, 0)

            group_weights = tuple((take_group(item) for item in weights))
            inflow, outflow, passed = level_sweep(
                arriving,
                group_weights,
                take_group(lateral_now),
                live_mask,
                one_hot,
                take_group(prev_in),
                take_group(prev_out),
            )
            inflow_keep = lax.dynamic_update_slice_in_dim(inflow_keep, inflow, first_row, 0)
            outflow_keep = lax.dynamic_update_slice_in_dim(outflow_keep, outflow, first_row, 0)
            return (passed, inflow_keep, outflow_keep)

        def skipped(operands):
            return (jnp.zeros_like(operands[0]), operands[1], operands[2])

        passed, inflow_all, outflow_all = lax.cond(
            active, compute, skipped, (incoming, inflow_all, outflow_all)
        )
        return (mover(passed), inflow_all, outflow_all)

    initial = (
        jnp.zeros((group_size, level_blocks, lane_count), jnp.float32),
        jnp.zeros_like(prev_in),
        jnp.zeros_like(prev_out),
    )
    _, inflow_all, outflow_all = lax.fori_loop(0, basins + groups - 1, advance, initial)
    return (inflow_all, outflow_all)


def shards(
    prior_params,
    lateral_flow,
    inflow_start,
    outflow_start,
    reach_count,
    downstream,
    gauge_reach,
    observed,
    obs_var,
    obs_noise,
):
    members_dev, param_count, block_dev = prior_params.shape
    lane_count = LANES
    level_blocks = BLK_LEV
    level_count = block_dev // level_blocks
    hour_count = lateral_flow.shape[1]
    lane_ids = jnp.arange(lane_count, dtype=jnp.int32)
    live_mask = (lane_ids[None, :] < reach_count[:, None]).astype(jnp.float32)
    targets = jnp.arange(level_blocks, dtype=jnp.int32)
    one_hot = [
        (
            downstream[None, level_idx * level_blocks : (level_idx + 1) * level_blocks]
            == targets[:, None]
        ).astype(jnp.float32)
        for level_idx in range(level_count)
    ]
    weight_now, weight_back, weight_carry = route_coefficients(prior_params)
    scaling = lateral_scaling(prior_params, lane_count)
    weights = (weight_now, weight_back, weight_carry, scaling)
    lateral_grid = lateral_flow.reshape(members_dev, hour_count, block_dev, lane_count)
    prev_in = jnp.broadcast_to(
        (inflow_start.reshape(block_dev, lane_count) * live_mask)[None],
        (members_dev, block_dev, lane_count),
    )
    prev_out = jnp.broadcast_to(
        (outflow_start.reshape(block_dev, lane_count) * live_mask)[None],
        (members_dev, block_dev, lane_count),
    )
    results = []
    for hour_idx in range(hour_count):
        lateral_now = lateral_grid[:, hour_idx]
        prev_in, prev_out = route_hour(
            lambda passed: shifted(passed, "basin", 1),
            4,
            weights,
            lateral_now,
            live_mask,
            one_hot,
            prev_in,
            prev_out,
        )
        flat = prev_out.reshape(members_dev, block_dev * lane_count)
        results.append(inverse_sinh(jnp.take(flat, gauge_reach, axis=1)))
    predicted = jnp.stack(results, 1)
    members = members_dev * lax.axis_size("member")
    spread = jnp.sqrt(obs_var)
    spread_root = math.sqrt(members - 1.0)
    innovation = (observed + 2.0 * spread * obs_noise - predicted) / (2.0 * spread)
    mean_pred = lax.psum(jnp.sum(predicted, 0), "member") / members
    scaled = (predicted - mean_pred) / (spread_root * (2.0 * spread))
    scaled_all, innov_all = (
        lax.all_gather(scaled, "member", axis=0, tiled=True),
        lax.all_gather(innovation, "member", axis=0, tiled=True),
    )
    scaled_rows = scaled_all.reshape(members, -1)
    innov_rows = innov_all.reshape(members, -1)
    gram_part = jnp.dot(
        scaled_rows, scaled_rows.T, precision=exact_mode, preferred_element_type=jnp.float32
    )
    cross_part = jnp.dot(
        scaled_rows, innov_rows.T, precision=exact_mode, preferred_element_type=jnp.float32
    )
    gram_matrix, cross_matrix = lax.psum((gram_part, cross_part), "basin")
    gram_matrix = gram_matrix + jnp.eye(members, dtype=jnp.float32)
    solved = solve_gram(gram_matrix, cross_matrix)
    prior_all = lax.all_gather(prior_params, "member", axis=0, tiled=True)
    mean_prior = jnp.sum(prior_all, 0) / members
    anomaly = (prior_all - mean_prior) / spread_root
    own_cols = lax.dynamic_slice_in_dim(
        solved, lax.axis_index("member") * members_dev, members_dev, 1
    )
    posterior = prior_params + jnp.einsum("mn,mkb->nkb", own_cols, anomaly, precision=exact_mode)
    return (posterior, predicted)


def solution(mesh):
    return jax.shard_map(
        shards,
        mesh=mesh,
        in_specs=(
            P("member", None, "basin"),
            P("member", None, "basin"),
            P("basin"),
            P("basin"),
            P("basin"),
            P("basin"),
            P("basin"),
            P(None, "basin"),
            P(None, "basin"),
            P("member", None, "basin"),
        ),
        out_specs=(P("member", None, "basin"), P("member", None, "basin")),
        check_vma=False,
    )
```

profile of v0, /device:TPU:0, one launch (start us, length us, event | category | flops | bytes accessed | tf_op | source)
XLA Modules:
  0.0 468.4 jit_solution(3943242846933802712)
XLA Ops:
  12.6 6.6 %reshape.277 = f32[32,2,128,128]{3,2,1,0:T(8,128)} reshape(f32[32,2,16384]{2,1,0:T(2,128)} %param.21) | data formatting | bytes 8388608 | tf_op jit(solution)/shard_map/reshape | solution.py:152
  19.2 4.9 %slice_bitcast_fusion.13 = (f32[32,128,128]{2,1,0:T(8,128)}, f32[32,128,128]{2,1,0:T(8,128)}) fusion(f32[32,2,128,128]{3,2,1,0:T(8,128)} %reshape.277), kind=kLoop, calls=%fused_computation.78 | loop fusion | bytes 8388608 | tf_op jit(solution)/shard_map/squeeze | solution.py:163
  31.5 106.7 %while.39 = (s32[]{:T(128)}, f32[8,64,128]{2,1,0:T(8,128)S(1)}, f32[32,128,128]{2,1,0:T(8,128)}, f32[32,128,128]{2,1,0:T(8,128)}, s32[]{:T(128)}, /*index=5*/f32...) while((s32[]{:T(128)}, f32[8,64,128]{2,1,0:T(8,128)S(1)}, ...), condition=%wide.region_3.4_spmd.clone, body=%wide.region_0.3_spmd.clone.sunk | while | flops 102023184 | bytes 7075321 | solution.py:118
  33.0 5.8 %conditional.6 = (f32[8,64,128]{2,1,0:T(8,128)S(1)}, f32[32,128,128]{2,1,0:T(8,128)}, f32[32,128,128]{2,1,0:T(8,128)}) conditional(s32[]{:T(128)} %convert_element_type.73, (f32[32,128,128]{2,1,0:T(8,128)}, f32[32,128,128]{2,1,0:T(8,128)}) %tuple.149, (s32[]{:T(128)}, f32[32,128,1]{1,0,2:T(8,128)S(1)}, f32[128,128]{1,0:T(8,128)S(1)}, ...), branch_computations={%region_1.1_spmd, %region_2.2_spmd} | conditional | flops 101974024 | bytes 5927046 | solution.py:108
  40.1 6.5 %collective-permute-done = f32[8,64,128]{2,1,0:T(8,128)S(1)} collective-permute-done((f32[8,64,128]{2,1,0:T(8,128)S(1)}, f32[8,64,128]{2,1,0:T(8,128)S(1)}, u32[]{:S(2)}, u32[]{:S(2)}) %collective-permute-start) | collective-permute-done | bytes 262176 | tf_op jit(solution)/shard_map/while/body/eval_jaxpr/ppermute | solution.py:15
  47.9 5.7 %conditional.6 = (f32[8,64,128]{2,1,0:T(8,128)S(1)}, f32[32,128,128]{2,1,0:T(8,128)}, f32[32,128,128]{2,1,0:T(8,128)}) conditional(s32[]{:T(128)} %convert_element_type.73, (f32[32,128,128]{2,1,0:T(8,128)}, f32[32,128,128]{2,1,0:T(8,128)}) %tuple.149, (s32[]{:T(128)}, f32[32,128,1]{1,0,2:T(8,128)S(1)}, f32[128,128]{1,0:T(8,128)S(1)}, ...), branch_computations={%region_1.1_spmd, %region_2.2_spmd} | conditional | flops 101974024 | bytes 5927046 | solution.py:108
  53.7 4.4 collective-permute-start
  58.1 5.6 %collective-permute-done = f32[8,64,128]{2,1,0:T(8,128)S(1)} collective-permute-done((f32[8,64,128]{2,1,0:T(8,128)S(1)}, f32[8,64,128]{2,1,0:T(8,128)S(1)}, u32[]{:S(2)}, u32[]{:S(2)}) %collective-permute-start) | collective-permute-done | bytes 262176 | tf_op jit(solution)/shard_map/while/body/eval_jaxpr/ppermute | solution.py:15
  65.2 5.8 %conditional.6 = (f32[8,64,128]{2,1,0:T(8,128)S(1)}, f32[32,128,128]{2,1,0:T(8,128)}, f32[32,128,128]{2,1,0:T(8,128)}) conditional(s32[]{:T(128)} %convert_element_type.73, (f32[32,128,128]{2,1,0:T(8,128)}, f32[32,128,128]{2,1,0:T(8,128)}) %tuple.149, (s32[]{:T(128)}, f32[32,128,1]{1,0,2:T(8,128)S(1)}, f32[128,128]{1,0:T(8,128)S(1)}, ...), branch_computations={%region_1.1_spmd, %region_2.2_spmd} | conditional | flops 101974024 | bytes 5927046 | solution.py:108
  70.9 4.4 collective-permute-start
  75.3 4.8 %collective-permute-done = f32[8,64,128]{2,1,0:T(8,128)S(1)} collective-permute-done((f32[8,64,128]{2,1,0:T(8,128)S(1)}, f32[8,64,128]{2,1,0:T(8,128)S(1)}, u32[]{:S(2)}, u32[]{:S(2)}) %collective-permute-start) | collective-permute-done | bytes 262176 | tf_op jit(solution)/shard_map/while/body/eval_jaxpr/ppermute | solution.py:15
  81.5 5.8 %conditional.6 = (f32[8,64,128]{2,1,0:T(8,128)S(1)}, f32[32,128,128]{2,1,0:T(8,128)}, f32[32,128,128]{2,1,0:T(8,128)}) conditional(s32[]{:T(128)} %convert_element_type.73, (f32[32,128,128]{2,1,0:T(8,128)}, f32[32,128,128]{2,1,0:T(8,128)}) %tuple.149, (s32[]{:T(128)}, f32[32,128,1]{1,0,2:T(8,128)S(1)}, f32[128,128]{1,0:T(8,128)S(1)}, ...), branch_computations={%region_1.1_spmd, %region_2.2_spmd} | conditional | flops 101974024 | bytes 5927046 | solution.py:108
  87.3 4.4 collective-permute-start
  91.7 3.9 collective-permute-done
  97.1 10.3 %collective-permute-start = (f32[8,64,128]{2,1,0:T(8,128)S(1)}, f32[8,64,128]{2,1,0:T(8,128)S(1)}, u32[]{:S(2)}, u32[]{:S(2)}) collective-permute-start(f32[8,64,128]{2,1,0:T(8,128)S(1)} %get-tuple-element.1072), channel_id=1, source_target_pairs={{0,1},{1,2},{2,3},{4,5},{5,6},{6,7},{8,9},{9,10},{10,11},{12,13},{... | collective-permute-start | bytes 786440 | tf_op jit(solution)/shard_map/while/body/eval_jaxpr/ppermute | solution.py:15
  107.4 3.9 collective-permute-done
  112.7 5.3 %collective-permute-start = (f32[8,64,128]{2,1,0:T(8,128)S(1)}, f32[8,64,128]{2,1,0:T(8,128)S(1)}, u32[]{:S(2)}, u32[]{:S(2)}) collective-permute-start(f32[8,64,128]{2,1,0:T(8,128)S(1)} %get-tuple-element.1072), channel_id=1, source_target_pairs={{0,1},{1,2},{2,3},{4,5},{5,6},{6,7},{8,9},{9,10},{10,11},{12,13},{... | collective-permute-start | bytes 786440 | tf_op jit(solution)/shard_map/while/body/eval_jaxpr/ppermute | solution.py:15
  118.0 3.9 collective-permute-done
  123.4 11.0 %collective-permute-start = (f32[8,64,128]{2,1,0:T(8,128)S(1)}, f32[8,64,128]{2,1,0:T(8,128)S(1)}, u32[]{:S(2)}, u32[]{:S(2)}) collective-permute-start(f32[8,64,128]{2,1,0:T(8,128)S(1)} %get-tuple-element.1072), channel_id=1, source_target_pairs={{0,1},{1,2},{2,3},{4,5},{5,6},{6,7},{8,9},{9,10},{10,11},{12,13},{... | collective-permute-start | bytes 786440 | tf_op jit(solution)/shard_map/while/body/eval_jaxpr/ppermute | solution.py:15
  134.4 3.9 collective-permute-done
  138.2 6.4 %copy.30 = f32[32,128,128]{0,2,1:T(8,128)} copy(f32[32,128,128]{2,1,0:T(8,128)} %get-tuple-element.1167) | data formatting | bytes 4194304 | tf_op jit(solution)/shard_map/while | solution.py:118
  146.2 98.9 %while.40 = (s32[]{:T(128)}, f32[8,64,128]{2,1,0:T(8,128)S(1)}, f32[32,128,128]{2,1,0:T(8,128)}, s32[]{:T(128)}, f32[32,128,1]{1,0,2:T(8,128)S(1)}, /*index=5*/f...) while((s32[]{:T(128)}, f32[8,64,128]{2,1,0:T(8,128)S(1)}, ...), condition=%wide.region_7.9_spmd.clone, body=%wide.region_4.8_spmd.clone.sunk | while | flops 101892112 | bytes 6157773 | solution.py:118
  147.7 5.1 %conditional.7 = (f32[8,64,128]{2,1,0:T(8,128)S(1)}, f32[32,128,128]{2,1,0:T(8,128)}) conditional(s32[]{:T(128)} %convert_element_type.76, f32[32,128,128]{2,1,0:T(8,128)} %get-tuple-element.1176, (s32[]{:T(128)}, f32[32,128,1]{1,0,2:T(8,128)S(1)}, f32[128,128]{1,0:T(8,128)S(1)}, f32[32,128,128]{2,1,0:T(8,128)}, f32[32,128,128]{2,1,0:T(8,128)S(1)}, ...), branch_computations={%region_5.6_spmd, %region_6.7_spmd} | conditional | flops 101842952 | bytes 5009530 | solution.py:108
  154.1 3.9 collective-permute-done.1
  159.4 5.1 %conditional.7 = (f32[8,64,128]{2,1,0:T(8,128)S(1)}, f32[32,128,128]{2,1,0:T(8,128)}) conditional(s32[]{:T(128)} %convert_element_type.76, f32[32,128,128]{2,1,0:T(8,128)} %get-tuple-element.1176, (s32[]{:T(128)}, f32[32,128,1]{1,0,2:T(8,128)S(1)}, f32[128,128]{1,0:T(8,128)S(1)}, f32[32,128,128]{2,1,0:T(8,128)}, f32[32,128,128]{2,1,0:T(8,128)S(1)}, ...), branch_computations={%region_5.6_spmd, %region_6.7_spmd} | conditional | flops 101842952 | bytes 5009530 | solution.py:108
  164.5 5.7 %collective-permute-start.1 = (f32[8,64,128]{2,1,0:T(8,128)S(1)}, f32[8,64,128]{2,1,0:T(8,128)S(1)}, u32[]{:S(2)}, u32[]{:S(2)}) collective-permute-start(f32[8,64,128]{2,1,0:T(8,128)S(1)} %get-tuple-element.1091), channel_id=1, source_target_pairs={{0,1},{1,2},{2,3},{4,5},{5,6},{6,7},{8,9},{9,10},{10,11},{12,13},{... | collective-permute-start | bytes 786440 | tf_op jit(solution)/shard_map/while/body/eval_jaxpr/ppermute | solution.py:15
  175.5 5.1 %conditional.7 = (f32[8,64,128]{2,1,0:T(8,128)S(1)}, f32[32,128,128]{2,1,0:T(8,128)}) conditional(s32[]{:T(128)} %convert_element_type.76, f32[32,128,128]{2,1,0:T(8,128)} %get-tuple-element.1176, (s32[]{:T(128)}, f32[32,128,1]{1,0,2:T(8,128)S(1)}, f32[128,128]{1,0:T(8,128)S(1)}, f32[32,128,128]{2,1,0:T(8,128)}, f32[32,128,128]{2,1,0:T(8,128)S(1)}, ...), branch_computations={%region_5.6_spmd, %region_6.7_spmd} | conditional | flops 101842952 | bytes 5009530 | solution.py:108
  180.6 4.4 collective-permute-start.1
  190.3 5.1 %conditional.7 = (f32[8,64,128]{2,1,0:T(8,128)S(1)}, f32[32,128,128]{2,1,0:T(8,128)}) conditional(s32[]{:T(128)} %convert_element_type.76, f32[32,128,128]{2,1,0:T(8,128)} %get-tuple-element.1176, (s32[]{:T(128)}, f32[32,128,1]{1,0,2:T(8,128)S(1)}, f32[128,128]{1,0:T(8,128)S(1)}, f32[32,128,128]{2,1,0:T(8,128)}, f32[32,128,128]{2,1,0:T(8,128)S(1)}, ...), branch_computations={%region_5.6_spmd, %region_6.7_spmd} | conditional | flops 101842952 | bytes 5009530 | solution.py:108
  195.5 4.4 collective-permute-start.1
  205.2 9.5 %collective-permute-start.1 = (f32[8,64,128]{2,1,0:T(8,128)S(1)}, f32[8,64,128]{2,1,0:T(8,128)S(1)}, u32[]{:S(2)}, u32[]{:S(2)}) collective-permute-start(f32[8,64,128]{2,1,0:T(8,128)S(1)} %get-tuple-element.1091), channel_id=1, source_target_pairs={{0,1},{1,2},{2,3},{4,5},{5,6},{6,7},{8,9},{9,10},{10,11},{12,13},{... | collective-permute-start | bytes 786440 | tf_op jit(solution)/shard_map/while/body/eval_jaxpr/ppermute | solution.py:15
  214.7 5.5 %collective-permute-done.1 = f32[8,64,128]{2,1,0:T(8,128)S(1)} collective-permute-done((f32[8,64,128]{2,1,0:T(8,128)S(1)}, f32[8,64,128]{2,1,0:T(8,128)S(1)}, u32[]{:S(2)}, u32[]{:S(2)}) %collective-permute-start.1) | collective-permute-done | bytes 262176 | tf_op jit(solution)/shard_map/while/body/eval_jaxpr/ppermute | solution.py:15
  221.7 4.4 collective-permute-start.1
  226.1 4.6 collective-permute-done.1
  232.2 9.1 %collective-permute-start.1 = (f32[8,64,128]{2,1,0:T(8,128)S(1)}, f32[8,64,128]{2,1,0:T(8,128)S(1)}, u32[]{:S(2)}, u32[]{:S(2)}) collective-permute-start(f32[8,64,128]{2,1,0:T(8,128)S(1)} %get-tuple-element.1091), channel_id=1, source_target_pairs={{0,1},{1,2},{2,3},{4,5},{5,6},{6,7},{8,9},{9,10},{10,11},{12,13},{... | collective-permute-start | bytes 786440 | tf_op jit(solution)/shard_map/while/body/eval_jaxpr/ppermute | solution.py:15
  245.2 6.3 %copy.32 = f32[32,128,128]{0,2,1:T(8,128)} copy(f32[32,128,128]{2,1,0:T(8,128)} %get-tuple-element.648) | data formatting | bytes 4194304 | tf_op jit(solution)/shard_map/while | solution.py:118
  251.5 4.4 gather_fusion.1
  256.0 4.4 gather_fusion
  261.4 13.6 %psum.21 = f32[2,512]{1,0:T(2,128)S(1)} all-reduce(f32[2,512]{1,0:T(2,128)S(1)} %get-tuple-element.849), channel_id=1, replica_groups=mesh['member'=8,'basin'=4] {'member'}, use_global_device_ids=true, to_apply=%region_9.11 | all-reduce | flops 1024 | bytes 8192 | tf_op jit(solution)/shard_map/psum | solution.py:181
  277.4 23.8 %all-gather.4.cloned.1.call-done = f32[256,2,512]{2,0,1:T(8,128)} async-done(((f32[32,2,512]{2,0,1:T(8,128)}), f32[256,2,512]{2,0,1:T(8,128)}) %all-gather.4.cloned.1.call-update) | async-done | bytes 1048592 | tf_op jit(solution)/shard_map/all_gather | solution.py:184
  304.5 20.7 %all-gather.6.cloned.1.call-done = f32[256,2,512]{2,0,1:T(8,128)} async-done(((f32[32,2,512]{2,0,1:T(8,128)}), f32[256,2,512]{2,0,1:T(8,128)}) %all-gather.6.cloned.1.call-update) | async-done | bytes 1048592 | tf_op jit(solution)/shard_map/all_gather | solution.py:185
  329.0 19.7 %all-gather.8.cloned.1.call-done = f32[256,8,128]{2,1,0:T(8,128)} async-done(((f32[32,8,128]{2,1,0:T(8,128)}), f32[256,8,128]{2,1,0:T(8,128)}) %all-gather.8.cloned.1.call-update) | async-done | bytes 1048592 | tf_op jit(solution)/shard_map/all_gather | solution.py:198
  351.5 45.1 %all-reduce.4.cloned.1.call-done = (f32[256,256]{1,0:T(8,128)}, f32[256,256]{0,1:T(8,128)}) async-done(((f32[256,256]{1,0:T(8,128)}, f32[256,256]{0,1:T(8,128)}), (f32[256,256]{1,0:T(8,128)}, f32[256,256]{0,1:T(8,128)})) %all-reduce.4.cloned.1.call-update) | async-done | bytes 524304 | tf_op jit(solution)/shard_map/psum | solution.py:195
  398.7 11.7 %cholesky.49 = f32[128,128]{1,0:T(8,128)S(1)} custom-call(f32[128,128]{1,0:T(8,128)S(1)} %cholesky.115), custom_call_target="Cholesky" | custom-call | tf_op jit(solution)/shard_map/jit(cholesky)/cholesky | solution.py:43
  410.5 9.8 %custom-call.16 = f32[1,128,128]{1,2,0:T(8,128)S(1)} custom-call(f32[1,128,128]{2,1,0:T(8,128)S(1)} %get-tuple-element.857), custom_call_target="InvertDiagBlocksLowerTriangular" | custom-call | tf_op jit(solution)/shard_map/jit(cholesky)/cholesky | solution.py:43
  420.8 11.9 %cholesky.102 = f32[128,128]{1,0:T(8,128)S(1)} custom-call(f32[128,128]{1,0:T(8,128)S(1)} %convolution_subtract_fusion.2), custom_call_target="Cholesky" | custom-call | tf_op jit(solution)/shard_map/jit(cholesky)/cholesky | solution.py:43
  434.8 3.9 while.38
  438.7 19.7 %custom-call.17 = f32[2,128,128]{1,2,0:T(8,128)S(1)} custom-call(f32[2,128,128]{2,1,0:T(8,128)S(1)} %get-tuple-element.656), custom_call_target="InvertDiagBlocksLowerTriangular" | custom-call | tf_op jit(solution)/shard_map/triangular_solve | solution.py:45
  (224 shorter events, 119.5 us)
Async XLA Ops:
  7.2 294.0 %all-gather.4.cloned.1.call-start = ((), (), s32[]{:S(2)}) async-start(), calls=%async_computation | async-start | bytes 1179648 | tf_op jit(solution)/shard_map/all_gather | solution.py:184
  19.2 4.9 %copy-start.1 = (f32[32,8,128]{2,1,0:T(8,128)S(1)}, f32[32,8,128]{2,1,0:T(8,128)}, u32[]{:S(2)}) copy-start(f32[32,8,128]{2,1,0:T(8,128)} %param.20) | copy-start | bytes 393220
  24.1 3.5 copy-start.5
  24.1 3.5 copy-start.6
  38.7 7.8 %collective-permute-start = (f32[8,64,128]{2,1,0:T(8,128)S(1)}, f32[8,64,128]{2,1,0:T(8,128)S(1)}, u32[]{:S(2)}, u32[]{:S(2)}) collective-permute-start(f32[8,64,128]{2,1,0:T(8,128)S(1)} %get-tuple-element.1072), channel_id=1, source_target_pairs={{0,1},{1,2},{2,3},{4,5},{5,6},{6,7},{8,9},{9,10},{10,11},{12,13},{... | collective-permute-start | bytes 786440 | tf_op jit(solution)/shard_map/while/body/eval_jaxpr/ppermute | solution.py:15
  53.7 10.0 %collective-permute-start = (f32[8,64,128]{2,1,0:T(8,128)S(1)}, f32[8,64,128]{2,1,0:T(8,128)S(1)}, u32[]{:S(2)}, u32[]{:S(2)}) collective-permute-start(f32[8,64,128]{2,1,0:T(8,128)S(1)} %get-tuple-element.1072), channel_id=1, source_target_pairs={{0,1},{1,2},{2,3},{4,5},{5,6},{6,7},{8,9},{9,10},{10,11},{12,13},{... | collective-permute-start | bytes 786440 | tf_op jit(solution)/shard_map/while/body/eval_jaxpr/ppermute | solution.py:15
  70.9 9.2 %collective-permute-start = (f32[8,64,128]{2,1,0:T(8,128)S(1)}, f32[8,64,128]{2,1,0:T(8,128)S(1)}, u32[]{:S(2)}, u32[]{:S(2)}) collective-permute-start(f32[8,64,128]{2,1,0:T(8,128)S(1)} %get-tuple-element.1072), channel_id=1, source_target_pairs={{0,1},{1,2},{2,3},{4,5},{5,6},{6,7},{8,9},{9,10},{10,11},{12,13},{... | collective-permute-start | bytes 786440 | tf_op jit(solution)/shard_map/while/body/eval_jaxpr/ppermute | solution.py:15
  87.3 8.3 %collective-permute-start = (f32[8,64,128]{2,1,0:T(8,128)S(1)}, f32[8,64,128]{2,1,0:T(8,128)S(1)}, u32[]{:S(2)}, u32[]{:S(2)}) collective-permute-start(f32[8,64,128]{2,1,0:T(8,128)S(1)} %get-tuple-element.1072), channel_id=1, source_target_pairs={{0,1},{1,2},{2,3},{4,5},{5,6},{6,7},{8,9},{9,10},{10,11},{12,13},{... | collective-permute-start | bytes 786440 | tf_op jit(solution)/shard_map/while/body/eval_jaxpr/ppermute | solution.py:15
  97.1 14.2 %collective-permute-start = (f32[8,64,128]{2,1,0:T(8,128)S(1)}, f32[8,64,128]{2,1,0:T(8,128)S(1)}, u32[]{:S(2)}, u32[]{:S(2)}) collective-permute-start(f32[8,64,128]{2,1,0:T(8,128)S(1)} %get-tuple-element.1072), channel_id=1, source_target_pairs={{0,1},{1,2},{2,3},{4,5},{5,6},{6,7},{8,9},{9,10},{10,11},{12,13},{... | collective-permute-start | bytes 786440 | tf_op jit(solution)/shard_map/while/body/eval_jaxpr/ppermute | solution.py:15
  112.7 9.1 %collective-permute-start = (f32[8,64,128]{2,1,0:T(8,128)S(1)}, f32[8,64,128]{2,1,0:T(8,128)S(1)}, u32[]{:S(2)}, u32[]{:S(2)}) collective-permute-start(f32[8,64,128]{2,1,0:T(8,128)S(1)} %get-tuple-element.1072), channel_id=1, source_target_pairs={{0,1},{1,2},{2,3},{4,5},{5,6},{6,7},{8,9},{9,10},{10,11},{12,13},{... | collective-permute-start | bytes 786440 | tf_op jit(solution)/shard_map/while/body/eval_jaxpr/ppermute | solution.py:15
  123.4 14.9 %collective-permute-start = (f32[8,64,128]{2,1,0:T(8,128)S(1)}, f32[8,64,128]{2,1,0:T(8,128)S(1)}, u32[]{:S(2)}, u32[]{:S(2)}) collective-permute-start(f32[8,64,128]{2,1,0:T(8,128)S(1)} %get-tuple-element.1072), channel_id=1, source_target_pairs={{0,1},{1,2},{2,3},{4,5},{5,6},{6,7},{8,9},{9,10},{10,11},{12,13},{... | collective-permute-start | bytes 786440 | tf_op jit(solution)/shard_map/while/body/eval_jaxpr/ppermute | solution.py:15
  152.8 5.2 %collective-permute-start.1 = (f32[8,64,128]{2,1,0:T(8,128)S(1)}, f32[8,64,128]{2,1,0:T(8,128)S(1)}, u32[]{:S(2)}, u32[]{:S(2)}) collective-permute-start(f32[8,64,128]{2,1,0:T(8,128)S(1)} %get-tuple-element.1091), channel_id=1, source_target_pairs={{0,1},{1,2},{2,3},{4,5},{5,6},{6,7},{8,9},{9,10},{10,11},{12,13},{... | collective-permute-start | bytes 786440 | tf_op jit(solution)/shard_map/while/body/eval_jaxpr/ppermute | solution.py:15
  164.5 9.5 %collective-permute-start.1 = (f32[8,64,128]{2,1,0:T(8,128)S(1)}, f32[8,64,128]{2,1,0:T(8,128)S(1)}, u32[]{:S(2)}, u32[]{:S(2)}) collective-permute-start(f32[8,64,128]{2,1,0:T(8,128)S(1)} %get-tuple-element.1091), channel_id=1, source_target_pairs={{0,1},{1,2},{2,3},{4,5},{5,6},{6,7},{8,9},{9,10},{10,11},{12,13},{... | collective-permute-start | bytes 786440 | tf_op jit(solution)/shard_map/while/body/eval_jaxpr/ppermute | solution.py:15
  180.6 8.3 %collective-permute-start.1 = (f32[8,64,128]{2,1,0:T(8,128)S(1)}, f32[8,64,128]{2,1,0:T(8,128)S(1)}, u32[]{:S(2)}, u32[]{:S(2)}) collective-permute-start(f32[8,64,128]{2,1,0:T(8,128)S(1)} %get-tuple-element.1091), channel_id=1, source_target_pairs={{0,1},{1,2},{2,3},{4,5},{5,6},{6,7},{8,9},{9,10},{10,11},{12,13},{... | collective-permute-start | bytes 786440 | tf_op jit(solution)/shard_map/while/body/eval_jaxpr/ppermute | solution.py:15
  195.5 8.3 %collective-permute-start.1 = (f32[8,64,128]{2,1,0:T(8,128)S(1)}, f32[8,64,128]{2,1,0:T(8,128)S(1)}, u32[]{:S(2)}, u32[]{:S(2)}) collective-permute-start(f32[8,64,128]{2,1,0:T(8,128)S(1)} %get-tuple-element.1091), channel_id=1, source_target_pairs={{0,1},{1,2},{2,3},{4,5},{5,6},{6,7},{8,9},{9,10},{10,11},{12,13},{... | collective-permute-start | bytes 786440 | tf_op jit(solution)/shard_map/while/body/eval_jaxpr/ppermute | solution.py:15
  205.2 15.0 %collective-permute-start.1 = (f32[8,64,128]{2,1,0:T(8,128)S(1)}, f32[8,64,128]{2,1,0:T(8,128)S(1)}, u32[]{:S(2)}, u32[]{:S(2)}) collective-permute-start(f32[8,64,128]{2,1,0:T(8,128)S(1)} %get-tuple-element.1091), channel_id=1, source_target_pairs={{0,1},{1,2},{2,3},{4,5},{5,6},{6,7},{8,9},{9,10},{10,11},{12,13},{... | collective-permute-start | bytes 786440 | tf_op jit(solution)/shard_map/while/body/eval_jaxpr/ppermute | solution.py:15
  221.7 9.1 %collective-permute-start.1 = (f32[8,64,128]{2,1,0:T(8,128)S(1)}, f32[8,64,128]{2,1,0:T(8,128)S(1)}, u32[]{:S(2)}, u32[]{:S(2)}) collective-permute-start(f32[8,64,128]{2,1,0:T(8,128)S(1)} %get-tuple-element.1091), channel_id=1, source_target_pairs={{0,1},{1,2},{2,3},{4,5},{5,6},{6,7},{8,9},{9,10},{10,11},{12,13},{... | collective-permute-start | bytes 786440 | tf_op jit(solution)/shard_map/while/body/eval_jaxpr/ppermute | solution.py:15
  232.2 12.9 %collective-permute-start.1 = (f32[8,64,128]{2,1,0:T(8,128)S(1)}, f32[8,64,128]{2,1,0:T(8,128)S(1)}, u32[]{:S(2)}, u32[]{:S(2)}) collective-permute-start(f32[8,64,128]{2,1,0:T(8,128)S(1)} %get-tuple-element.1091), channel_id=1, source_target_pairs={{0,1},{1,2},{2,3},{4,5},{5,6},{6,7},{8,9},{9,10},{10,11},{12,13},{... | collective-permute-start | bytes 786440 | tf_op jit(solution)/shard_map/while/body/eval_jaxpr/ppermute | solution.py:15
  245.2 6.3 %copy-start.7 = (s32[512]{0:T(512)S(1)}, s32[512]{0:T(512)}, u32[]{:S(2)}) copy-start(s32[512]{0:T(512)} %compare_select_fusion) | copy-start | bytes 6148
  245.2 15.4 %copy-start.9 = (f32[2,512]{1,0:T(2,128)S(1)}, f32[2,512]{1,0:T(2,128)}, u32[]{:S(2)}) copy-start(f32[2,512]{1,0:T(2,128)} %param.28) | copy-start | bytes 12292
  245.2 15.4 %copy-start.10 = (pred[512]{0:T(512)(128)(4,1)S(1)}, pred[512]{0:T(512)(128)(4,1)}, u32[]{:S(2)}) copy-start(pred[512]{0:T(512)(128)(4,1)} %compare_and_fusion) | copy-start | bytes 1540
  251.4 9.2 %copy-start.4 = (f32[32,2,512]{2,1,0:T(2,128)S(1)}, f32[32,2,512]{2,1,0:T(2,128)}, u32[]{:S(2)}) copy-start(f32[32,2,512]{2,1,0:T(2,128)} %param.29) | copy-start | bytes 393220
  251.4 9.2 %copy-start.8 = (f32[2,512]{1,0:T(2,128)S(1)}, f32[2,512]{1,0:T(2,128)}, u32[]{:S(2)}) copy-start(f32[2,512]{1,0:T(2,128)} %param.27) | copy-start | bytes 12292
  275.7 49.6 %all-gather.6.cloned.1.call-start = ((), (), s32[]{:S(2)}) async-start(), calls=%async_computation.1 | async-start | bytes 1179648 | tf_op jit(solution)/shard_map/all_gather | solution.py:185
  276.4 72.3 %all-gather.8.cloned.1.call-start = ((), (), s32[]{:S(2)}) async-start(), calls=%async_computation.2 | async-start | bytes 1179648 | tf_op jit(solution)/shard_map/all_gather | solution.py:198
  277.1 119.5 %all-reduce.4.cloned.1.call-start = ((), (), s32[]{:S(2)}) async-start(), calls=%async_computation.3 | async-start | bytes 1048576 | tf_op jit(solution)/shard_map/psum | solution.py:195
  301.2 24.1 %copy-start = (f32[256,2,512]{2,0,1:T(8,128)S(1)}, f32[256,2,512]{2,0,1:T(8,128)}, u32[]{:S(2)}) copy-start(f32[256,2,512]{2,0,1:T(8,128)} %all-gather.4.cloned.1.call-done) | copy-start | bytes 3145732
  397.6 60.8 %copy-start.3 = (f32[256,256]{1,0:T(8,128)S(1)}, f32[256,256]{1,0:T(8,128)}, u32[]{:S(2)}) copy-start(f32[256,256]{1,0:T(8,128)} %get-tuple-element.810) | copy-start | bytes 786436
  420.3 39.9 %copy-start.2 = (f32[32,8,128]{2,1,0:T(8,128)S(1)}, f32[32,8,128]{2,1,0:T(8,128)}, u32[]{:S(2)}) copy-start(f32[32,8,128]{2,1,0:T(8,128)} %param.20) | copy-start | bytes 393220
Sparse Core Ops, SparseCore 0:
  275.8 25.3 all-gather.3
  303.4 21.8 all-gather.5
  326.8 21.8 all-gather.7
  351.5 45.0 all-reduce.3
where the time goes:
time: 471 us; the launch traced here: 468 us
  waiting for transfers between devices  172 us (37%)
  other arithmetic  102 us (22%)
  starting transfers between devices  80.2 us (17%)
  local copies, waits for them, and re-layouts  56.3 us (12%)
  matrix products  27.6 us (6%)
  between operations  15.4 us (3%)
  blocking collectives  13.6 us (3%)
    ppermute x14, starting transfers between devices, shifted(): return lax.ppermute(block, axis, route)  79.8 us
    ppermute x14, waiting for transfers between devices, shifted(): return lax.ppermute(block, axis, route)  61.7 us
    psum x1, waiting for transfers between devices, shards(): gram_matrix, cross_matrix = lax.psum((gram_part, cross_part), 'basin')  45.1 us
    another operation x6, other arithmetic, solve_gram(): factor = jnp.linalg.cholesky(gram_matrix)  34.1 us
    all_gather x1, waiting for transfers between devices, shards(): lax.all_gather(scaled, 'member', axis=0, tiled=True)  23.8 us
    all_gather x1, waiting for transfers between devices, shards(): lax.all_gather(innovation, 'member', axis=0, tiled=True)  20.7 us
    another operation x3, other arithmetic, solve_gram(): lax.linalg.triangular_solve(factor, halfway, left_side=True, lower=True,...  19.7 us
    all_gather x1, waiting for transfers between devices, shards(): prior_all = lax.all_gather(prior_params, 'member', axis=0, tiled=True)  19.7 us
  transfers between devices with their start and end apart: 18, of which 18 were waited for; matrix products, arithmetic and copies ran while one was open for 2% of the time, Pallas kernels for 0%

commit v1 on v0

--- a/solution.py
+++ b/solution.py
@@ -7,6 +7,24 @@
 LANES = 128
 BLK_LEV = 64
 exact_mode = lax.Precision.HIGHEST
+
+
+def pack_halves_over_axis(field, array_dim):
+    s_next = list(field.shape[1:])
+    s_next[array_dim] *= field.shape[0]
+    return jnp.moveaxis(field, 0, array_dim).reshape(s_next)
+
+
+def change_threads_on_mesh(arr_in, row_axis):
+    nodes = lax.axis_size(row_axis)
+    before = arr_in[None]
+    for at in range(nodes.bit_length() - 1):
+        t1 = 1 << at
+        oldest = lax.ppermute(before, row_axis, [(nth, nth ^ t1) for nth in range(nodes)])
+        next_value = jnp.stack([before, oldest])
+        moved = lax.axis_index(row_axis) >> at & 1
+        before = jnp.where(moved == 0, next_value, next_value[::-1]).reshape(-1, *arr_in.shape)
+    return before
 
 
 def shifted(block, axis, distance):
@@ -131,6 +149,10 @@
     obs_var,
     obs_noise,
 ):
+
+    def track_the_fields(sample, raw, dim_at):
+        return pack_halves_over_axis(change_threads_on_mesh(sample, raw), dim_at)
+
     members_dev, param_count, block_dev = prior_params.shape
     lane_count = LANES
     level_blocks = BLK_LEV
@@ -181,7 +203,7 @@
     mean_pred = lax.psum(jnp.sum(predicted, 0), "member") / members
     scaled = (predicted - mean_pred) / (spread_root * (2.0 * spread))
     scaled_all, innov_all = (
-        lax.all_gather(scaled, "member", axis=0, tiled=True),
+        track_the_fields(scaled, "member", dim_at=0),
         lax.all_gather(innovation, "member", axis=0, tiled=True),
     )
     scaled_rows = scaled_all.reshape(members, -1)

time: 471 us -> 453 us (0.962)
  waiting for transfers between devices: 172 us -> 155 us
    ppermute x0 -> x3, waiting for transfers between devices: none -> 48.7 us  [change_threads_on_mesh(): lax.ppermute(before, row_axis, [(nth, nth ^ t1) for nth in range(nodes)])]
    all_gather x1 -> x0, waiting for transfers between devices: 23.8 us -> none  [shards(): lax.all_gather(scaled, 'member', axis=0, tiled=True)]
    all_gather x1, waiting for transfers between devices: 20.7 us -> 0.01 us  [shards(): lax.all_gather(innovation, 'member', axis=0, tiled=True)]
    all_gather x1, waiting for transfers between devices: 19.7 us -> 0.01 us  [shards(): prior_all = lax.all_gather(prior_params, 'member', axis=0, tiled=True)]
  transfers between devices with their start and end apart: 18 -> 20, of which waited for: 18 -> 18; matrix products, arithmetic and copies ran while one was open for 2% -> 2% of each run, Pallas kernels for 0% -> 0%
where the time goes in v1:
time: 453 us; the launch traced here: 451 us
  waiting for transfers between devices  155 us (34%)
  other arithmetic  101 us (22%)
  starting transfers between devices  80.4 us (18%)
  local copies, waits for them, and re-layouts  59.4 us (13%)
  matrix products  24.7 us (5%)
  between operations  15.5 us (3%)
  blocking collectives  13.6 us (3%)
    ppermute x14, starting transfers between devices, shifted(): return lax.ppermute(block, axis, route)  79.8 us
    ppermute x14, waiting for transfers between devices, shifted(): return lax.ppermute(block, axis, route)  61.7 us
    ppermute x3, waiting for transfers between devices, change_threads_on_mesh(): lax.ppermute(before, row_axis, [(nth, nth ^ t1) for nth in range(nodes)])  48.7 us
    psum x1, waiting for transfers between devices, shards(): gram_matrix, cross_matrix = lax.psum((gram_part, cross_part), 'basin')  44.3 us
    another operation x6, other arithmetic, solve_gram(): factor = jnp.linalg.cholesky(gram_matrix)  34.2 us
    another operation x3, other arithmetic, solve_gram(): lax.linalg.triangular_solve(factor, halfway, left_side=True, lower=True,...  19.7 us
    dot_general x16, matrix products, level_sweep(): jnp.einsum('nj,gjr->gnr', one_hot[level_idx], outflow, precision=exact_mode)  14.7 us
    psum x1, blocking collectives, shards(): mean_pred = lax.psum(jnp.sum(predicted, 0), 'member') / members  13.6 us
  transfers between devices with their start and end apart: 20, of which 18 were waited for; matrix products, arithmetic and copies ran while one was open for 2% of the time, Pallas kernels for 0%

profile of v1, /device:TPU:0, one launch (start us, length us, event | category | flops | bytes accessed | tf_op | source)
XLA Modules:
  0.0 451.1 jit_solution(17639809582739261375)
XLA Ops:
  12.6 6.6 %reshape.353 = f32[32,2,128,128]{3,2,1,0:T(8,128)} reshape(f32[32,2,16384]{2,1,0:T(2,128)} %param.21) | data formatting | bytes 8388608 | tf_op jit(solution)/shard_map/reshape | solution.py:174
  19.2 4.9 %slice_bitcast_fusion.13 = (f32[32,128,128]{2,1,0:T(8,128)}, f32[32,128,128]{2,1,0:T(8,128)}) fusion(f32[32,2,128,128]{3,2,1,0:T(8,128)} %reshape.353), kind=kLoop, calls=%fused_computation.78 | loop fusion | bytes 8388608 | tf_op jit(solution)/shard_map/squeeze | solution.py:185
  31.5 106.7 %while.39 = (s32[]{:T(128)}, f32[8,64,128]{2,1,0:T(8,128)S(1)}, f32[32,128,128]{2,1,0:T(8,128)}, f32[32,128,128]{2,1,0:T(8,128)}, s32[]{:T(128)}, /*index=5*/f32...) while((s32[]{:T(128)}, f32[8,64,128]{2,1,0:T(8,128)S(1)}, ...), condition=%wide.region_3.4_spmd.clone, body=%wide.region_0.3_spmd.clone.sunk | while | flops 102023184 | bytes 7075321 | solution.py:136
  33.0 5.8 %conditional.6 = (f32[8,64,128]{2,1,0:T(8,128)S(1)}, f32[32,128,128]{2,1,0:T(8,128)}, f32[32,128,128]{2,1,0:T(8,128)}) conditional(s32[]{:T(128)} %convert_element_type.73, (f32[32,128,128]{2,1,0:T(8,128)}, f32[32,128,128]{2,1,0:T(8,128)}) %tuple.159, (s32[]{:T(128)}, f32[32,128,1]{1,0,2:T(8,128)S(1)}, f32[128,128]{1,0:T(8,128)S(1)}, ...), branch_computations={%region_1.1_spmd, %region_2.2_spmd} | conditional | flops 101974024 | bytes 5927046 | solution.py:126
  40.1 6.5 %collective-permute-done = f32[8,64,128]{2,1,0:T(8,128)S(1)} collective-permute-done((f32[8,64,128]{2,1,0:T(8,128)S(1)}, f32[8,64,128]{2,1,0:T(8,128)S(1)}, u32[]{:S(2)}, u32[]{:S(2)}) %collective-permute-start) | collective-permute-done | bytes 262176 | tf_op jit(solution)/shard_map/while/body/eval_jaxpr/ppermute | solution.py:33
  47.9 5.7 %conditional.6 = (f32[8,64,128]{2,1,0:T(8,128)S(1)}, f32[32,128,128]{2,1,0:T(8,128)}, f32[32,128,128]{2,1,0:T(8,128)}) conditional(s32[]{:T(128)} %convert_element_type.73, (f32[32,128,128]{2,1,0:T(8,128)}, f32[32,128,128]{2,1,0:T(8,128)}) %tuple.159, (s32[]{:T(128)}, f32[32,128,1]{1,0,2:T(8,128)S(1)}, f32[128,128]{1,0:T(8,128)S(1)}, ...), branch_computations={%region_1.1_spmd, %region_2.2_spmd} | conditional | flops 101974024 | bytes 5927046 | solution.py:126
  53.7 4.4 collective-permute-start
  58.1 5.6 %collective-permute-done = f32[8,64,128]{2,1,0:T(8,128)S(1)} collective-permute-done((f32[8,64,128]{2,1,0:T(8,128)S(1)}, f32[8,64,128]{2,1,0:T(8,128)S(1)}, u32[]{:S(2)}, u32[]{:S(2)}) %collective-permute-start) | collective-permute-done | bytes 262176 | tf_op jit(solution)/shard_map/while/body/eval_jaxpr/ppermute | solution.py:33
  65.2 5.8 %conditional.6 = (f32[8,64,128]{2,1,0:T(8,128)S(1)}, f32[32,128,128]{2,1,0:T(8,128)}, f32[32,128,128]{2,1,0:T(8,128)}) conditional(s32[]{:T(128)} %convert_element_type.73, (f32[32,128,128]{2,1,0:T(8,128)}, f32[32,128,128]{2,1,0:T(8,128)}) %tuple.159, (s32[]{:T(128)}, f32[32,128,1]{1,0,2:T(8,128)S(1)}, f32[128,128]{1,0:T(8,128)S(1)}, ...), branch_computations={%region_1.1_spmd, %region_2.2_spmd} | conditional | flops 101974024 | bytes 5927046 | solution.py:126
  70.9 4.4 collective-permute-start
  75.3 4.8 %collective-permute-done = f32[8,64,128]{2,1,0:T(8,128)S(1)} collective-permute-done((f32[8,64,128]{2,1,0:T(8,128)S(1)}, f32[8,64,128]{2,1,0:T(8,128)S(1)}, u32[]{:S(2)}, u32[]{:S(2)}) %collective-permute-start) | collective-permute-done | bytes 262176 | tf_op jit(solution)/shard_map/while/body/eval_jaxpr/ppermute | solution.py:33
  81.5 5.8 %conditional.6 = (f32[8,64,128]{2,1,0:T(8,128)S(1)}, f32[32,128,128]{2,1,0:T(8,128)}, f32[32,128,128]{2,1,0:T(8,128)}) conditional(s32[]{:T(128)} %convert_element_type.73, (f32[32,128,128]{2,1,0:T(8,128)}, f32[32,128,128]{2,1,0:T(8,128)}) %tuple.159, (s32[]{:T(128)}, f32[32,128,1]{1,0,2:T(8,128)S(1)}, f32[128,128]{1,0:T(8,128)S(1)}, ...), branch_computations={%region_1.1_spmd, %region_2.2_spmd} | conditional | flops 101974024 | bytes 5927046 | solution.py:126
  87.3 4.4 collective-permute-start
  91.7 3.9 collective-permute-done
  97.1 10.3 %collective-permute-start = (f32[8,64,128]{2,1,0:T(8,128)S(1)}, f32[8,64,128]{2,1,0:T(8,128)S(1)}, u32[]{:S(2)}, u32[]{:S(2)}) collective-permute-start(f32[8,64,128]{2,1,0:T(8,128)S(1)} %get-tuple-element.1087), channel_id=1, source_target_pairs={{0,1},{1,2},{2,3},{4,5},{5,6},{6,7},{8,9},{9,10},{10,11},{12,13},{... | collective-permute-start | bytes 786440 | tf_op jit(solution)/shard_map/while/body/eval_jaxpr/ppermute | solution.py:33
  107.4 3.9 collective-permute-done
  112.7 5.3 %collective-permute-start = (f32[8,64,128]{2,1,0:T(8,128)S(1)}, f32[8,64,128]{2,1,0:T(8,128)S(1)}, u32[]{:S(2)}, u32[]{:S(2)}) collective-permute-start(f32[8,64,128]{2,1,0:T(8,128)S(1)} %get-tuple-element.1087), channel_id=1, source_target_pairs={{0,1},{1,2},{2,3},{4,5},{5,6},{6,7},{8,9},{9,10},{10,11},{12,13},{... | collective-permute-start | bytes 786440 | tf_op jit(solution)/shard_map/while/body/eval_jaxpr/ppermute | solution.py:33
  118.0 3.9 collective-permute-done
  123.4 11.0 %collective-permute-start = (f32[8,64,128]{2,1,0:T(8,128)S(1)}, f32[8,64,128]{2,1,0:T(8,128)S(1)}, u32[]{:S(2)}, u32[]{:S(2)}) collective-permute-start(f32[8,64,128]{2,1,0:T(8,128)S(1)} %get-tuple-element.1087), channel_id=1, source_target_pairs={{0,1},{1,2},{2,3},{4,5},{5,6},{6,7},{8,9},{9,10},{10,11},{12,13},{... | collective-permute-start | bytes 786440 | tf_op jit(solution)/shard_map/while/body/eval_jaxpr/ppermute | solution.py:33
  134.4 3.9 collective-permute-done
  138.2 6.4 %copy.88 = f32[32,128,128]{0,2,1:T(8,128)} copy(f32[32,128,128]{2,1,0:T(8,128)} %get-tuple-element.1182) | data formatting | bytes 4194304 | tf_op jit(solution)/shard_map/while | solution.py:136
  146.2 98.9 %while.40 = (s32[]{:T(128)}, f32[8,64,128]{2,1,0:T(8,128)S(1)}, f32[32,128,128]{2,1,0:T(8,128)}, s32[]{:T(128)}, f32[32,128,1]{1,0,2:T(8,128)S(1)}, /*index=5*/f...) while((s32[]{:T(128)}, f32[8,64,128]{2,1,0:T(8,128)S(1)}, ...), condition=%wide.region_7.9_spmd.clone, body=%wide.region_4.8_spmd.clone.sunk | while | flops 101892112 | bytes 6157773 | solution.py:136
  147.7 5.1 %conditional.7 = (f32[8,64,128]{2,1,0:T(8,128)S(1)}, f32[32,128,128]{2,1,0:T(8,128)}) conditional(s32[]{:T(128)} %convert_element_type.76, f32[32,128,128]{2,1,0:T(8,128)} %get-tuple-element.1191, (s32[]{:T(128)}, f32[32,128,1]{1,0,2:T(8,128)S(1)}, f32[128,128]{1,0:T(8,128)S(1)}, f32[32,128,128]{2,1,0:T(8,128)}, f32[32,128,128]{2,1,0:T(8,128)S(1)}, ...), branch_computations={%region_5.6_spmd, %region_6.7_spmd} | conditional | flops 101842952 | bytes 5009530 | solution.py:126
  154.1 3.9 collective-permute-done.1
  159.4 5.2 %conditional.7 = (f32[8,64,128]{2,1,0:T(8,128)S(1)}, f32[32,128,128]{2,1,0:T(8,128)}) conditional(s32[]{:T(128)} %convert_element_type.76, f32[32,128,128]{2,1,0:T(8,128)} %get-tuple-element.1191, (s32[]{:T(128)}, f32[32,128,1]{1,0,2:T(8,128)S(1)}, f32[128,128]{1,0:T(8,128)S(1)}, f32[32,128,128]{2,1,0:T(8,128)}, f32[32,128,128]{2,1,0:T(8,128)S(1)}, ...), branch_computations={%region_5.6_spmd, %region_6.7_spmd} | conditional | flops 101842952 | bytes 5009530 | solution.py:126
  164.6 5.6 %collective-permute-start.1 = (f32[8,64,128]{2,1,0:T(8,128)S(1)}, f32[8,64,128]{2,1,0:T(8,128)S(1)}, u32[]{:S(2)}, u32[]{:S(2)}) collective-permute-start(f32[8,64,128]{2,1,0:T(8,128)S(1)} %get-tuple-element.1106), channel_id=1, source_target_pairs={{0,1},{1,2},{2,3},{4,5},{5,6},{6,7},{8,9},{9,10},{10,11},{12,13},{... | collective-permute-start | bytes 786440 | tf_op jit(solution)/shard_map/while/body/eval_jaxpr/ppermute | solution.py:33
  170.2 3.9 collective-permute-done.1
  175.5 5.1 %conditional.7 = (f32[8,64,128]{2,1,0:T(8,128)S(1)}, f32[32,128,128]{2,1,0:T(8,128)}) conditional(s32[]{:T(128)} %convert_element_type.76, f32[32,128,128]{2,1,0:T(8,128)} %get-tuple-element.1191, (s32[]{:T(128)}, f32[32,128,1]{1,0,2:T(8,128)S(1)}, f32[128,128]{1,0:T(8,128)S(1)}, f32[32,128,128]{2,1,0:T(8,128)}, f32[32,128,128]{2,1,0:T(8,128)S(1)}, ...), branch_computations={%region_5.6_spmd, %region_6.7_spmd} | conditional | flops 101842952 | bytes 5009530 | solution.py:126
  180.6 4.4 collective-permute-start.1
  190.3 5.1 %conditional.7 = (f32[8,64,128]{2,1,0:T(8,128)S(1)}, f32[32,128,128]{2,1,0:T(8,128)}) conditional(s32[]{:T(128)} %convert_element_type.76, f32[32,128,128]{2,1,0:T(8,128)} %get-tuple-element.1191, (s32[]{:T(128)}, f32[32,128,1]{1,0,2:T(8,128)S(1)}, f32[128,128]{1,0:T(8,128)S(1)}, f32[32,128,128]{2,1,0:T(8,128)}, f32[32,128,128]{2,1,0:T(8,128)S(1)}, ...), branch_computations={%region_5.6_spmd, %region_6.7_spmd} | conditional | flops 101842952 | bytes 5009530 | solution.py:126
  195.5 4.4 collective-permute-start.1
  205.2 9.5 %collective-permute-start.1 = (f32[8,64,128]{2,1,0:T(8,128)S(1)}, f32[8,64,128]{2,1,0:T(8,128)S(1)}, u32[]{:S(2)}, u32[]{:S(2)}) collective-permute-start(f32[8,64,128]{2,1,0:T(8,128)S(1)} %get-tuple-element.1106), channel_id=1, source_target_pairs={{0,1},{1,2},{2,3},{4,5},{5,6},{6,7},{8,9},{9,10},{10,11},{12,13},{... | collective-permute-start | bytes 786440 | tf_op jit(solution)/shard_map/while/body/eval_jaxpr/ppermute | solution.py:33
  214.7 5.5 %collective-permute-done.1 = f32[8,64,128]{2,1,0:T(8,128)S(1)} collective-permute-done((f32[8,64,128]{2,1,0:T(8,128)S(1)}, f32[8,64,128]{2,1,0:T(8,128)S(1)}, u32[]{:S(2)}, u32[]{:S(2)}) %collective-permute-start.1) | collective-permute-done | bytes 262176 | tf_op jit(solution)/shard_map/while/body/eval_jaxpr/ppermute | solution.py:33
  221.7 4.4 collective-permute-start.1
  226.1 4.6 %collective-permute-done.1 = f32[8,64,128]{2,1,0:T(8,128)S(1)} collective-permute-done((f32[8,64,128]{2,1,0:T(8,128)S(1)}, f32[8,64,128]{2,1,0:T(8,128)S(1)}, u32[]{:S(2)}, u32[]{:S(2)}) %collective-permute-start.1) | collective-permute-done | bytes 262176 | tf_op jit(solution)/shard_map/while/body/eval_jaxpr/ppermute | solution.py:33
  232.2 9.1 %collective-permute-start.1 = (f32[8,64,128]{2,1,0:T(8,128)S(1)}, f32[8,64,128]{2,1,0:T(8,128)S(1)}, u32[]{:S(2)}, u32[]{:S(2)}) collective-permute-start(f32[8,64,128]{2,1,0:T(8,128)S(1)} %get-tuple-element.1106), channel_id=1, source_target_pairs={{0,1},{1,2},{2,3},{4,5},{5,6},{6,7},{8,9},{9,10},{10,11},{12,13},{... | collective-permute-start | bytes 786440 | tf_op jit(solution)/shard_map/while/body/eval_jaxpr/ppermute | solution.py:33
  245.2 6.3 %copy.90 = f32[32,128,128]{0,2,1:T(8,128)} copy(f32[32,128,128]{2,1,0:T(8,128)} %get-tuple-element.648) | data formatting | bytes 4194304 | tf_op jit(solution)/shard_map/while | solution.py:136
  251.5 4.4 gather_fusion.1
  256.0 4.4 gather_fusion
  261.6 13.6 %psum.21 = f32[2,512]{1,0:T(2,128)S(1)} all-reduce(f32[2,512]{1,0:T(2,128)S(1)} %get-tuple-element.857), channel_id=1, replica_groups=mesh['member'=8,'basin'=4] {'member'}, use_global_device_ids=true, to_apply=%region_9.11 | all-reduce | flops 1024 | bytes 8192 | tf_op jit(solution)/shard_map/psum | solution.py:203
  277.1 14.8 %collective-permute-done.3 = f32[2,32,2,512]{3,1,2,0:T(8,128)S(1)} collective-permute-done((f32[2,32,2,512]{3,1,2,0:T(8,128)S(1)}, f32[2,32,2,512]{3,1,2,0:T(8,128)S(1)}, u32[]{:S(2)}, u32[]{:S(2)}) %collective-permute-start.3) | collective-permute-done | bytes 262176 | tf_op jit(solution)/shard_map/ppermute | solution.py:23
  292.8 32.6 %collective-permute-done.4 = f32[4,32,2,512]{3,2,1,0:T(2,128)S(1)} collective-permute-done((f32[4,32,2,512]{3,2,1,0:T(2,128)S(1)}, f32[4,32,2,512]{3,2,1,0:T(2,128)S(1)}, u32[]{:S(2)}, u32[]{:S(2)}) %collective-permute-start.4) | collective-permute-done | bytes 524320 | tf_op jit(solution)/shard_map/ppermute | solution.py:23
  335.1 44.3 %all-reduce.4.cloned.1.call-done = (f32[256,256]{1,0:T(8,128)}, f32[256,256]{0,1:T(8,128)}) async-done(((f32[256,256]{1,0:T(8,128)}, f32[256,256]{0,1:T(8,128)}), (f32[256,256]{1,0:T(8,128)}, f32[256,256]{0,1:T(8,128)})) %all-reduce.4.cloned.1.call-update) | async-done | bytes 524304 | tf_op jit(solution)/shard_map/psum | solution.py:217
  381.5 11.7 %cholesky.49 = f32[128,128]{1,0:T(8,128)S(1)} custom-call(f32[128,128]{1,0:T(8,128)S(1)} %cholesky.115), custom_call_target="Cholesky" | custom-call | tf_op jit(solution)/shard_map/jit(cholesky)/cholesky | solution.py:61
  393.3 9.8 %custom-call.16 = f32[1,128,128]{1,2,0:T(8,128)S(1)} custom-call(f32[1,128,128]{2,1,0:T(8,128)S(1)} %get-tuple-element.871), custom_call_target="InvertDiagBlocksLowerTriangular" | custom-call | tf_op jit(solution)/shard_map/jit(cholesky)/cholesky | solution.py:61
  403.6 11.9 %cholesky.102 = f32[128,128]{1,0:T(8,128)S(1)} custom-call(f32[128,128]{1,0:T(8,128)S(1)} %convolution_subtract_fusion.2), custom_call_target="Cholesky" | custom-call | tf_op jit(solution)/shard_map/jit(cholesky)/cholesky | solution.py:61
  417.6 3.9 while.38
  421.5 19.7 %custom-call.17 = f32[2,128,128]{1,2,0:T(8,128)S(1)} custom-call(f32[2,128,128]{2,1,0:T(8,128)S(1)} %get-tuple-element.656), custom_call_target="InvertDiagBlocksLowerTriangular" | custom-call | tf_op jit(solution)/shard_map/triangular_solve | solution.py:63
  (237 shorter events, 115.9 us)
Async XLA Ops:
  7.2 321.2 %all-gather.3.cloned.1.call-start = ((), (), s32[]{:S(2)}) async-start(), calls=%async_computation | async-start | bytes 1179648 | tf_op jit(solution)/shard_map/all_gather | solution.py:207
  19.2 4.9 %copy-start = (f32[32,8,128]{2,1,0:T(8,128)S(1)}, f32[32,8,128]{2,1,0:T(8,128)}, u32[]{:S(2)}) copy-start(f32[32,8,128]{2,1,0:T(8,128)} %param.20) | copy-start | bytes 393220
  24.1 3.5 copy-start.4
  24.1 3.5 copy-start.5
  38.7 7.8 %collective-permute-start = (f32[8,64,128]{2,1,0:T(8,128)S(1)}, f32[8,64,128]{2,1,0:T(8,128)S(1)}, u32[]{:S(2)}, u32[]{:S(2)}) collective-permute-start(f32[8,64,128]{2,1,0:T(8,128)S(1)} %get-tuple-element.1087), channel_id=1, source_target_pairs={{0,1},{1,2},{2,3},{4,5},{5,6},{6,7},{8,9},{9,10},{10,11},{12,13},{... | collective-permute-start | bytes 786440 | tf_op jit(solution)/shard_map/while/body/eval_jaxpr/ppermute | solution.py:33
  53.7 10.0 %collective-permute-start = (f32[8,64,128]{2,1,0:T(8,128)S(1)}, f32[8,64,128]{2,1,0:T(8,128)S(1)}, u32[]{:S(2)}, u32[]{:S(2)}) collective-permute-start(f32[8,64,128]{2,1,0:T(8,128)S(1)} %get-tuple-element.1087), channel_id=1, source_target_pairs={{0,1},{1,2},{2,3},{4,5},{5,6},{6,7},{8,9},{9,10},{10,11},{12,13},{... | collective-permute-start | bytes 786440 | tf_op jit(solution)/shard_map/while/body/eval_jaxpr/ppermute | solution.py:33
  70.9 9.2 %collective-permute-start = (f32[8,64,128]{2,1,0:T(8,128)S(1)}, f32[8,64,128]{2,1,0:T(8,128)S(1)}, u32[]{:S(2)}, u32[]{:S(2)}) collective-permute-start(f32[8,64,128]{2,1,0:T(8,128)S(1)} %get-tuple-element.1087), channel_id=1, source_target_pairs={{0,1},{1,2},{2,3},{4,5},{5,6},{6,7},{8,9},{9,10},{10,11},{12,13},{... | collective-permute-start | bytes 786440 | tf_op jit(solution)/shard_map/while/body/eval_jaxpr/ppermute | solution.py:33
  87.3 8.3 %collective-permute-start = (f32[8,64,128]{2,1,0:T(8,128)S(1)}, f32[8,64,128]{2,1,0:T(8,128)S(1)}, u32[]{:S(2)}, u32[]{:S(2)}) collective-permute-start(f32[8,64,128]{2,1,0:T(8,128)S(1)} %get-tuple-element.1087), channel_id=1, source_target_pairs={{0,1},{1,2},{2,3},{4,5},{5,6},{6,7},{8,9},{9,10},{10,11},{12,13},{... | collective-permute-start | bytes 786440 | tf_op jit(solution)/shard_map/while/body/eval_jaxpr/ppermute | solution.py:33
  97.1 14.2 %collective-permute-start = (f32[8,64,128]{2,1,0:T(8,128)S(1)}, f32[8,64,128]{2,1,0:T(8,128)S(1)}, u32[]{:S(2)}, u32[]{:S(2)}) collective-permute-start(f32[8,64,128]{2,1,0:T(8,128)S(1)} %get-tuple-element.1087), channel_id=1, source_target_pairs={{0,1},{1,2},{2,3},{4,5},{5,6},{6,7},{8,9},{9,10},{10,11},{12,13},{... | collective-permute-start | bytes 786440 | tf_op jit(solution)/shard_map/while/body/eval_jaxpr/ppermute | solution.py:33
  112.7 9.1 %collective-permute-start = (f32[8,64,128]{2,1,0:T(8,128)S(1)}, f32[8,64,128]{2,1,0:T(8,128)S(1)}, u32[]{:S(2)}, u32[]{:S(2)}) collective-permute-start(f32[8,64,128]{2,1,0:T(8,128)S(1)} %get-tuple-element.1087), channel_id=1, source_target_pairs={{0,1},{1,2},{2,3},{4,5},{5,6},{6,7},{8,9},{9,10},{10,11},{12,13},{... | collective-permute-start | bytes 786440 | tf_op jit(solution)/shard_map/while/body/eval_jaxpr/ppermute | solution.py:33
  123.4 14.9 %collective-permute-start = (f32[8,64,128]{2,1,0:T(8,128)S(1)}, f32[8,64,128]{2,1,0:T(8,128)S(1)}, u32[]{:S(2)}, u32[]{:S(2)}) collective-permute-start(f32[8,64,128]{2,1,0:T(8,128)S(1)} %get-tuple-element.1087), channel_id=1, source_target_pairs={{0,1},{1,2},{2,3},{4,5},{5,6},{6,7},{8,9},{9,10},{10,11},{12,13},{... | collective-permute-start | bytes 786440 | tf_op jit(solution)/shard_map/while/body/eval_jaxpr/ppermute | solution.py:33
  152.8 5.2 %collective-permute-start.1 = (f32[8,64,128]{2,1,0:T(8,128)S(1)}, f32[8,64,128]{2,1,0:T(8,128)S(1)}, u32[]{:S(2)}, u32[]{:S(2)}) collective-permute-start(f32[8,64,128]{2,1,0:T(8,128)S(1)} %get-tuple-element.1106), channel_id=1, source_target_pairs={{0,1},{1,2},{2,3},{4,5},{5,6},{6,7},{8,9},{9,10},{10,11},{12,13},{... | collective-permute-start | bytes 786440 | tf_op jit(solution)/shard_map/while/body/eval_jaxpr/ppermute | solution.py:33
  164.6 9.5 %collective-permute-start.1 = (f32[8,64,128]{2,1,0:T(8,128)S(1)}, f32[8,64,128]{2,1,0:T(8,128)S(1)}, u32[]{:S(2)}, u32[]{:S(2)}) collective-permute-start(f32[8,64,128]{2,1,0:T(8,128)S(1)} %get-tuple-element.1106), channel_id=1, source_target_pairs={{0,1},{1,2},{2,3},{4,5},{5,6},{6,7},{8,9},{9,10},{10,11},{12,13},{... | collective-permute-start | bytes 786440 | tf_op jit(solution)/shard_map/while/body/eval_jaxpr/ppermute | solution.py:33
  180.6 8.3 %collective-permute-start.1 = (f32[8,64,128]{2,1,0:T(8,128)S(1)}, f32[8,64,128]{2,1,0:T(8,128)S(1)}, u32[]{:S(2)}, u32[]{:S(2)}) collective-permute-start(f32[8,64,128]{2,1,0:T(8,128)S(1)} %get-tuple-element.1106), channel_id=1, source_target_pairs={{0,1},{1,2},{2,3},{4,5},{5,6},{6,7},{8,9},{9,10},{10,11},{12,13},{... | collective-permute-start | bytes 786440 | tf_op jit(solution)/shard_map/while/body/eval_jaxpr/ppermute | solution.py:33
  195.5 8.3 %collective-permute-start.1 = (f32[8,64,128]{2,1,0:T(8,128)S(1)}, f32[8,64,128]{2,1,0:T(8,128)S(1)}, u32[]{:S(2)}, u32[]{:S(2)}) collective-permute-start(f32[8,64,128]{2,1,0:T(8,128)S(1)} %get-tuple-element.1106), channel_id=1, source_target_pairs={{0,1},{1,2},{2,3},{4,5},{5,6},{6,7},{8,9},{9,10},{10,11},{12,13},{... | collective-permute-start | bytes 786440 | tf_op jit(solution)/shard_map/while/body/eval_jaxpr/ppermute | solution.py:33
  205.2 15.0 %collective-permute-start.1 = (f32[8,64,128]{2,1,0:T(8,128)S(1)}, f32[8,64,128]{2,1,0:T(8,128)S(1)}, u32[]{:S(2)}, u32[]{:S(2)}) collective-permute-start(f32[8,64,128]{2,1,0:T(8,128)S(1)} %get-tuple-element.1106), channel_id=1, source_target_pairs={{0,1},{1,2},{2,3},{4,5},{5,6},{6,7},{8,9},{9,10},{10,11},{12,13},{... | collective-permute-start | bytes 786440 | tf_op jit(solution)/shard_map/while/body/eval_jaxpr/ppermute | solution.py:33
  221.7 9.0 %collective-permute-start.1 = (f32[8,64,128]{2,1,0:T(8,128)S(1)}, f32[8,64,128]{2,1,0:T(8,128)S(1)}, u32[]{:S(2)}, u32[]{:S(2)}) collective-permute-start(f32[8,64,128]{2,1,0:T(8,128)S(1)} %get-tuple-element.1106), channel_id=1, source_target_pairs={{0,1},{1,2},{2,3},{4,5},{5,6},{6,7},{8,9},{9,10},{10,11},{12,13},{... | collective-permute-start | bytes 786440 | tf_op jit(solution)/shard_map/while/body/eval_jaxpr/ppermute | solution.py:33
  232.2 12.9 %collective-permute-start.1 = (f32[8,64,128]{2,1,0:T(8,128)S(1)}, f32[8,64,128]{2,1,0:T(8,128)S(1)}, u32[]{:S(2)}, u32[]{:S(2)}) collective-permute-start(f32[8,64,128]{2,1,0:T(8,128)S(1)} %get-tuple-element.1106), channel_id=1, source_target_pairs={{0,1},{1,2},{2,3},{4,5},{5,6},{6,7},{8,9},{9,10},{10,11},{12,13},{... | collective-permute-start | bytes 786440 | tf_op jit(solution)/shard_map/while/body/eval_jaxpr/ppermute | solution.py:33
  245.2 6.3 %copy-start.6 = (s32[512]{0:T(512)S(1)}, s32[512]{0:T(512)}, u32[]{:S(2)}) copy-start(s32[512]{0:T(512)} %compare_select_fusion) | copy-start | bytes 6148
  245.2 15.4 %copy-start.8 = (f32[2,512]{1,0:T(2,128)S(1)}, f32[2,512]{1,0:T(2,128)}, u32[]{:S(2)}) copy-start(f32[2,512]{1,0:T(2,128)} %param.28) | copy-start | bytes 12292
  245.2 15.4 %copy-start.9 = (pred[512]{0:T(512)(128)(4,1)S(1)}, pred[512]{0:T(512)(128)(4,1)}, u32[]{:S(2)}) copy-start(pred[512]{0:T(512)(128)(4,1)} %compare_and_fusion) | copy-start | bytes 1540
  251.5 9.2 %copy-start.3 = (f32[32,2,512]{2,1,0:T(2,128)S(1)}, f32[32,2,512]{2,1,0:T(2,128)}, u32[]{:S(2)}) copy-start(f32[32,2,512]{2,1,0:T(2,128)} %param.29) | copy-start | bytes 393220
  251.5 9.2 %copy-start.7 = (f32[2,512]{1,0:T(2,128)S(1)}, f32[2,512]{1,0:T(2,128)}, u32[]{:S(2)}) copy-start(f32[2,512]{1,0:T(2,128)} %param.27) | copy-start | bytes 12292
  261.5 70.7 %all-gather.5.cloned.1.call-start = ((), (), s32[]{:S(2)}) async-start(), calls=%async_computation.1 | async-start | bytes 1179648 | tf_op jit(solution)/shard_map/all_gather | solution.py:220
  275.2 1.4 collective-permute-start.2
  276.7 15.1 %collective-permute-start.3 = (f32[2,32,2,512]{3,1,2,0:T(8,128)S(1)}, f32[2,32,2,512]{3,1,2,0:T(8,128)S(1)}, u32[]{:S(2)}, u32[]{:S(2)}) collective-permute-start(f32[2,32,2,512]{3,1,2,0:T(8,128)S(1)} %get-tuple-element.855), channel_id=1, source_target_pairs={{0,8},{4,12},{8,0},{12,4},{16,24},{20,28},{24,16},{28,20},{1,9},{5... | collective-permute-start | bytes 786440 | tf_op jit(solution)/shard_map/ppermute | solution.py:23
  276.8 102.5 %all-reduce.4.cloned.1.call-start = ((), (), s32[]{:S(2)}) async-start(), calls=%async_computation.2 | async-start | bytes 1048576 | tf_op jit(solution)/shard_map/psum | solution.py:217
  292.3 33.1 %collective-permute-start.4 = (f32[4,32,2,512]{3,2,1,0:T(2,128)S(1)}, f32[4,32,2,512]{3,2,1,0:T(2,128)S(1)}, u32[]{:S(2)}, u32[]{:S(2)}) collective-permute-start(f32[4,32,2,512]{3,2,1,0:T(2,128)S(1)} %copy.94), channel_id=1, source_target_pairs={{0,16},{4,20},{8,24},{12,28},{16,0},{20,4},{24,8},{28,12},{1,17},{... | collective-permute-start | bytes 1572872 | tf_op jit(solution)/shard_map/ppermute | solution.py:23
  380.3 60.8 %copy-start.2 = (f32[256,256]{1,0:T(8,128)S(1)}, f32[256,256]{1,0:T(8,128)}, u32[]{:S(2)}) copy-start(f32[256,256]{1,0:T(8,128)} %get-tuple-element.816) | copy-start | bytes 786436
  403.1 39.9 %copy-start.1 = (f32[32,8,128]{2,1,0:T(8,128)S(1)}, f32[32,8,128]{2,1,0:T(8,128)}, u32[]{:S(2)}) copy-start(f32[32,8,128]{2,1,0:T(8,128)} %param.20) | copy-start | bytes 393220
Sparse Core Ops, SparseCore 0:
  261.7 31.9 all-gather.2
  295.2 25.1 all-gather.4
  331.6 47.6 all-reduce.3
